TPU v7x, 32 devices: a whole 2x2x4 slice. The times are simulated.
32 devices in a mesh: grp: 2 (over x), tile: 16 (over z, y, core).
Axes of the slice: x: 2, y: 2, z: 4, core: 2. Of those that a mesh axis runs over, the one named last changes fastest.
Arguments:
- visibility: bfloat16 [32, 16, 2, 256, 256], P('tile', 'grp'), parts along dimension 1, may hold values from -12 to 12
- station_beam: bfloat16 [16, 2, 512, 2048], P('grp', None, 'tile'), parts along dimension 0, may hold values from -4.1875 to 4.1875
- antenna_uvw: float32 [16, 3, 2048], P('grp'), parts along dimension 0, may hold values from -40 to 40
- source_dirs: float32 [2, 4096], P(None, 'tile'), may hold values from -0.4 to 0.4
- source_flux: bfloat16 [8192], P(('grp', 'tile')), parts along dimension 0, may hold values from 0.0029907227 to 0.029907227
- visible_list: int32 [8, 512], P(None, 'tile'), may hold values from 0 to 255
- antenna_flags: int32 [16, 2048], P('grp'), parts along dimension 0, may hold values 0 or 1
Outputs:
- residual: bfloat16 [32, 16, 2, 256, 256], P('tile', 'grp'), parts along dimension 1
- flux_grad: float32 [16, 512], P('grp', 'tile'), parts along dimension 0
There are 2 independent parts, one for each index of `grp`. A program takes and returns all parts, laid end to end along the dimension named above; an argument that names none is the same for every part. Nothing has to cross between parts.
Inputs may be any that keep to these rules, and one draw needn't show every extreme that they name: `visible_list`: entry k of a slot names pool source 256 * (k // 32) + value, a source of its own group. `antenna_flags`: 1 marks a flagged antenna.
All inputs are finite; a program needn't handle non-finite values.
Results may differ from a plain program's by a relative error of at most 0.0034.
Values may be sent and summed in bfloat16 or wider, within the bound.
A program may use at most 192 MiB of HBM per device.

v0:
```python
import math
import jax
import jax.numpy as jnp
import numpy as np
from jax import lax
from jax.sharding import PartitionSpec as P

BLOCKS = 8
two_pi = 2.0 * math.pi


def unit_table(block_count):
    first_list = []
    second_list = []
    diag_list = []
    for row_block in range(block_count):
        for col_block in range(row_block + 1, block_count):
            first_list.append(row_block)
            second_list.append(col_block)
            diag_list.append(0)
    for pair_index in range(block_count // 2):
        first_list.append(2 * pair_index)
        second_list.append(2 * pair_index + 1)
        diag_list.append(1)
    return (
        np.array(first_list, np.int32),
        np.array(second_list, np.int32),
        np.array(diag_list, np.int32),
    )


def build_factors(station_beam, antenna_uvw, source_dirs, source_flux, visible_list):
    pool_size = source_dirs.shape[1]
    chosen = visible_list[:, :, None] == jnp.arange(pool_size, dtype=jnp.int32)[None, None, :]
    coord_east = jnp.sum(jnp.where(chosen, source_dirs[0][None, None, :], 0.0), axis=2)
    coord_north = jnp.sum(jnp.where(chosen, source_dirs[1][None, None, :], 0.0), axis=2)
    brightness = jnp.sum(
        jnp.where(chosen, source_flux.astype(jnp.float32)[None, None, :], 0.0), axis=2
    ).astype(jnp.bfloat16)
    depth_term = jnp.sqrt(1.0 - coord_east * coord_east - coord_north * coord_north) - 1.0
    delay_sum = (
        antenna_uvw[:, 0, None, :] * coord_east[:, :, None]
        + antenna_uvw[:, 1, None, :] * coord_north[:, :, None]
        + antenna_uvw[:, 2, None, :] * depth_term[:, :, None]
    )
    phases = two_pi * delay_sum
    cosine = jnp.cos(phases)
    sine = jnp.sin(phases)
    beam_f = station_beam.astype(jnp.float32)
    real_part = beam_f[:, 0] * cosine + beam_f[:, 1] * sine
    imag_part = beam_f[:, 1] * cosine - beam_f[:, 0] * sine
    return (jnp.stack([real_part, imag_part], 1).astype(jnp.bfloat16), brightness)


def predict(rows_f, cols_f, brightness):
    scaled = (rows_f.astype(jnp.float32) * brightness.astype(jnp.float32)[:, None, :, None]).astype(
        jnp.bfloat16
    )
    turned = jnp.stack([scaled[:, 1], -scaled[:, 0]], 1)
    stacked = jnp.stack([scaled, turned], 1)
    return jnp.einsum("tdckr,tckq->tdrq", stacked, cols_f, preferred_element_type=jnp.float32)


def pull_back(resid, rows_f, cols_f):
    rstack = jnp.stack(
        [jnp.stack([resid[:, 0], -resid[:, 1]], 1), jnp.stack([resid[:, 1], resid[:, 0]], 1)], 1
    )
    pulled = jnp.einsum("tdcrq,tckq->tdkr", rstack, cols_f, preferred_element_type=jnp.float32)
    return jnp.sum(rows_f.astype(jnp.float32) * pulled, axis=(1, 3))


def unit_work(block_one, block_two, diag_tile, bright_all, vis_unit, keep_one, keep_two):
    span = vis_unit.shape[3]
    local_ids = jnp.arange(span, dtype=jnp.int32)
    upper_part = local_ids[:, None] < local_ids[None, :]
    lower_part = local_ids[:, None] > local_ids[None, :]
    cols_one = jnp.where(diag_tile, block_one, block_two)
    first_pred = predict(block_one, cols_one, bright_all)
    pred_shape = first_pred.shape
    second_pred = lax.cond(
        diag_tile,
        lambda: predict(block_two, block_two, bright_all),
        lambda: jnp.zeros(pred_shape, jnp.float32),
    )
    first_mask = jnp.logical_or(jnp.logical_not(diag_tile), upper_part)
    predicted = jnp.where(first_mask[None, None], first_pred, jnp.swapaxes(second_pred, 2, 3))
    upper_f = upper_part.astype(jnp.float32)
    lower_f = lower_part.astype(jnp.float32)
    off_weight = keep_one[:, :, None] * keep_two[:, None, :]
    diag_weight = (
        upper_f[None] * keep_one[:, :, None] * keep_one[:, None, :]
        + lower_f[None] * keep_two[:, :, None] * keep_two[:, None, :]
    )
    weights = jnp.where(diag_tile, diag_weight, off_weight)
    residual = (weights[:, None] * (vis_unit.astype(jnp.float32) - predicted)).astype(jnp.bfloat16)
    zero_res = jnp.zeros_like(residual)
    first_res = jnp.where(first_mask[None, None], residual, zero_res)
    partial_value = pull_back(first_res, block_one, cols_one)
    second_sel = jnp.logical_and(diag_tile, lower_part)
    grad_shape = partial_value.shape
    second_part = lax.cond(
        diag_tile,
        lambda: pull_back(
            jnp.swapaxes(jnp.where(second_sel[None, None], residual, zero_res), 2, 3),
            block_two,
            block_two,
        ),
        lambda: jnp.zeros(grad_shape, jnp.float32),
    )
    return (residual, partial_value + second_part)


def per_device(
    visibility, station_beam, antenna_uvw, source_dirs, source_flux, visible_list, antenna_flags
):
    tile_count = lax.axis_size("tile")
    units_dev = visibility.shape[0]
    span = visibility.shape[4]
    slot_count = station_beam.shape[0]
    per_group = station_beam.shape[2]
    antennas = station_beam.shape[3]
    tile_index = lax.axis_index("tile")
    first_tab, second_tab, diag_tab = unit_table(BLOCKS)
    first_arr = jnp.asarray(first_tab)
    second_arr = jnp.asarray(second_tab)
    diag_arr = jnp.asarray(diag_tab)
    keep_all = 1.0 - antenna_flags.astype(jnp.float32)
    owned, brightness = build_factors(
        station_beam, antenna_uvw, source_dirs, source_flux, visible_list
    )
    gathered, bright_all = (
        lax.all_gather(owned, "tile", axis=2, tiled=True),
        lax.all_gather(brightness, "tile", axis=1, tiled=True),
    )
    residuals = []
    partial_total = jnp.zeros((slot_count, per_group * tile_count), jnp.float32)
    for unit_slot in range(units_dev):
        unit_id = tile_index * units_dev + unit_slot
        start_one = (first_arr[unit_id] * span).astype(jnp.int32)
        start_two = (second_arr[unit_id] * span).astype(jnp.int32)
        diag_tile = diag_arr[unit_id] == 1
        block_one = lax.dynamic_slice_in_dim(gathered, start_one, span, 3)
        block_two = lax.dynamic_slice_in_dim(gathered, start_two, span, 3)
        keep_one = lax.dynamic_slice_in_dim(keep_all, start_one, span, 1)
        keep_two = lax.dynamic_slice_in_dim(keep_all, start_two, span, 1)
        residual, partial_value = unit_work(
            block_one, block_two, diag_tile, bright_all, visibility[unit_slot], keep_one, keep_two
        )
        residuals.append(residual)
        partial_total = partial_total + partial_value
    summed = lax.psum_scatter(partial_total, "tile", scatter_dimension=1, tiled=True)
    flux_grad = summed * (-1.0 / (8.0 * antennas))
    return (jnp.stack(residuals, 0), flux_grad)


def solution(mesh):
    return jax.shard_map(
        per_device,
        mesh=mesh,
        in_specs=(
            P("tile", "grp", None, None, None),
            P("grp", None, "tile", None),
            P("grp", None, None),
            P(None, "tile"),
            P(("grp", "tile")),
            P(None, "tile"),
            P("grp", None),
        ),
        out_specs=(P("tile", "grp", None, None, None), P("grp", "tile")),
        check_vma=False,
    )
```

profile of v0, /device:TPU:0, one launch (start us, length us, event | category | flops | bytes accessed | tf_op | source)
XLA Modules:
  0.0 425.8 jit_solution(3471020011920112316)
XLA Ops:
  9.6 2.1 convert_element_type.106
  12.0 8.9 %add_convert_fusion = (bf16[8,1,32,2048]{3,2,1,0:T(8,128)(2,1)S(1)}, bf16[8,1,32,2048]{3,2,1,0:T(8,128)(2,1)S(1)}) fusion(f32[8,2,32,2048]{3,2,1,0:T(8,128)S(1)} %convert_element_type.106, f32[8,32]{1,0:T(8,128)S(1)} %sqrt_add_fusion, f32[8,2048]{1,0:T(8,128)S(1)} %get-tuple-element.134, f32[8,32]{1,0:T(8,128)S(1)} %get-tuple-element.95, ...), kind=kLoop, calls=%fused_computation.93 | loop fusion | flops 7340032 | bytes 6491136 | tf_op jit(solution)/shard_map/convert.2
  21.2 2.5 copy.115
  29.1 23.9 %all-gather = bf16[16,32,8]{1,2,0:T(8,128)(2,1)S(1)} all-gather(bf16[1,32,8]{1,2,0:T(8,128)(2,1)S(1)} %bitcast.185), channel_id=1, replica_groups=mesh['grp'=2,'tile'=16] {'tile'}, dimensions={0}, use_global_device_ids=true | all-gather | bytes 8704 | tf_op jit(solution)/shard_map/all_gather | solution.py:133
  53.4 2.7 multiply_select_fusion.1
  56.1 138.6 %all-gather.3.cloned.1.call-done = bf16[8,2,512,2048]{3,0,1,2:T(8,128)(2,1)} async-done(((bf16[8,2,32,2048]{3,0,1,2:T(8,128)(2,1)}), bf16[8,2,512,2048]{3,0,1,2:T(8,128)(2,1)}) %all-gather.3.cloned.1.call-update) | async-done | bytes 33554448 | tf_op jit(solution)/shard_map/all_gather | solution.py:132
  194.7 12.4 %constant_dynamic-slice_fusion.5 = (bf16[8,2,512,256]{3,0,1,2:T(8,128)(2,1)}, bf16[8,2,512,256]{3,0,1,2:T(8,128)(2,1)}, bf16[8,2,512,256]{3,0,1,2:T(8,128)(2,1)}, bf16[8,2,512,256]{3,0,1,2:T(8,128)(2,1)}) fusion(bf16[8,2,512,2048]{3,0,1,2:T(8,128)(2,1)} %all-gather.3.cloned.1.call-done, s32[]{:T(128)S(6)} %select_n.94, s32[]{:T(128)S(6)} %select_n.105, ...), kind=kLoop, calls=%fused_computation.123 | loop fusion | bytes 33554448 | tf_op jit(solution)/shard_map/dynamic_slice | solution.py:142
  207.1 7.6 %copy.167 = bf16[8,2,512,256]{2,3,1,0:T(8,128)(2,1)} copy(bf16[8,2,512,256]{3,0,1,2:T(8,128)(2,1)} %get-tuple-element.111) | data formatting | bytes 8388608
  214.7 7.6 %copy.169 = bf16[8,2,512,256]{2,3,1,0:T(8,128)(2,1)} copy(bf16[8,2,512,256]{3,0,1,2:T(8,128)(2,1)} %get-tuple-element.112) | data formatting | bytes 8388608
  222.3 7.5 %fusion.44 = (bf16[8,2,512,256]{2,3,1,0:T(8,128)(2,1)S(1)}, bf16[8,2,512,256]{2,3,1,0:T(8,128)(2,1)}) fusion(bf16[8,2,512,256]{2,3,1,0:T(8,128)(2,1)} %copy.167, f32[8,512]{1,0:T(8,128)S(1)} %bitcast_convert_fusion, bf16[8,2,512,256]{2,3,1,0:T(8,128)(2,1)} %copy.169), kind=kLoop, calls=%fused_computation.50 | loop fusion | flops 12582912 | bytes 16793600 | tf_op jit(solution)/shard_map/convert_element_type | solution.py:56
  229.8 1.9 fusion.91
  232.4 7.6 %copy.168 = bf16[8,2,512,256]{2,3,1,0:T(8,128)(2,1)} copy(bf16[8,2,512,256]{3,0,1,2:T(8,128)(2,1)} %get-tuple-element.113) | data formatting | bytes 8388608
  240.1 2.5 conditional.4
  240.1 2.5 broadcast.220
  242.5 5.4 %copy.121 = f32[8,2,256,256]{2,3,1,0:T(8,128)} copy(f32[8,2,256,256]{3,2,1,0:T(8,128)} %get-tuple-element.156) | data formatting | bytes 8388608 | tf_op jit(solution)/shard_map/cond | solution.py:80
  248.0 4.3 %maximum_bitcast_fusion.6 = bf16[8,1,2,512,256]{3,4,2,1,0:T(8,128)(2,1)} fusion(bf16[8,1,512,256]{2,3,1,0:T(8,128)(2,1)} %get-tuple-element.118, bf16[8,1,512,256]{2,3,1,0:T(8,128)(2,1)S(1)} %get-tuple-element.117), kind=kLoop, calls=%fused_computation.61 | loop fusion | flops 2097152 | bytes 8388608 | tf_op jit(solution)/shard_map/stack | solution.py:60
  253.6 8.4 %broadcast_select_fusion.3 = (bf16[8,2,256,256]{3,2,1,0:T(8,128)(2,1)S(1)}, bf16[8,2,256,256]{3,2,1,0:T(8,128)(2,1)}) fusion(pred[256,256]{1,0:T(8,128)(4,1)S(1)} %fusion.85, f32[8,2,256,256]{2,3,1,0:T(8,128)} %copy.121, bf16[8,2,512,256]{2,3,1,0:T(8,128)(2,1)S(1)} %copy-done.6, bf16[8,2,512,256]{2,3,1,0:T(8,128)(2,1)S(1)} %copy-done, pred[]{:T(512)} %bitcast.28, ...), kind=kOutput, calls=%fused_computation.99 | convolution fusion | flops 2160066560 | bytes 29425664 | tf_op jit(solution)/shard_map/tdckr,tckq->tdrq/dot_general | solution.py:61
  262.0 1.8 slice_negate_fusion.7
  265.3 1.6 fusion.92
  266.9 7.5 %copy.170 = bf16[8,2,512,256]{2,3,1,0:T(8,128)(2,1)} copy(bf16[8,2,512,256]{3,0,1,2:T(8,128)(2,1)} %get-tuple-element.114) | data formatting | bytes 8388608
  274.4 2.5 conditional.5
  274.4 2.5 broadcast.221
  276.9 5.3 %copy.126 = f32[8,2,256,256]{2,3,1,0:T(8,128)} copy(f32[8,2,256,256]{3,2,1,0:T(8,128)} %get-tuple-element.157) | data formatting | bytes 8388608 | tf_op jit(solution)/shard_map/cond | solution.py:80
  282.2 4.3 %maximum_bitcast_fusion.7 = bf16[8,1,2,512,256]{3,4,2,0,1:T(8,128)(2,1)} fusion(bf16[8,1,512,256]{2,3,1,0:T(8,128)(2,1)} %get-tuple-element.120, bf16[8,1,512,256]{2,3,1,0:T(8,128)(2,1)S(1)} %get-tuple-element.119), kind=kLoop, calls=%fused_computation.62 | loop fusion | flops 2097152 | bytes 8388608 | tf_op jit(solution)/shard_map/stack | solution.py:60
  287.8 8.8 %broadcast_select_fusion.2 = (bf16[8,2,256,256]{3,2,1,0:T(8,128)(2,1)S(1)}, bf16[8,2,256,256]{3,2,1,0:T(8,128)(2,1)}) fusion(pred[256,256]{1,0:T(8,128)(4,1)S(1)} %fusion.84, f32[8,2,256,256]{2,3,1,0:T(8,128)} %copy.126, bf16[8,2,512,256]{2,3,1,0:T(8,128)(2,1)S(1)} %copy-done.4, bf16[8,2,512,256]{2,3,1,0:T(8,128)(2,1)} %copy.170, pred[]{:T(512)} %bitcast.48, ...), kind=kOutput, calls=%fused_computation.98 | convolution fusion | flops 2160066560 | bytes 29425664 | tf_op jit(solution)/shard_map/tdckr,tckq->tdrq/dot_general | solution.py:61
  296.6 1.8 slice_negate_fusion.6
  299.6 4.5 %maximum_bitcast_fusion.8 = (bf16[8,1,2,256,256]{4,3,2,0,1:T(8,128)(2,1)}, bf16[8,1,2,256,256]{4,3,2,0,1:T(8,128)(2,1)}) fusion(bf16[8,1,256,256]{3,2,1,0:T(8,128)(2,1)S(1)} %copy-done.10, bf16[8,1,256,256]{3,2,1,0:T(8,128)(2,1)} %get-tuple-element.123, bf16[8,1,256,256]{3,2,1,0:T(8,128)(2,1)} %get-tuple-element.122), kind=kLoop, calls=%fused_computation.87 | loop fusion | flops 2097152 | bytes 7340032 | tf_op jit(solution)/shard_map/stack | solution.py:65
  304.2 6.4 %fusion.45 = f32[8,512]{1,0:T(8,128)S(1)} fusion(bf16[8,2,512,256]{2,3,1,0:T(8,128)(2,1)} %copy.167, bf16[8,2,512,256]{2,3,1,0:T(8,128)(2,1)S(1)} %copy-done.1, pred[]{:T(512)} %bitcast.28, bf16[8,1,2,256,256]{4,3,2,0,1:T(8,128)(2,1)} %get-tuple-element.128, bf16[8,1,2,256,256]{4,3,2,0,1:T(8,128)(2,1)} %get-tuple-element.127), kind=kOutput, calls=%fused_computation.51 | convolution fusion | flops 2157965312 | bytes 12599297 | tf_op jit(solution)/shard_map/tdcrq,tckq->tdkr/dot_general | solution.py:68
  310.7 4.1 maximum_bitcast_fusion.10
  314.8 6.4 %fusion.47 = f32[8,512]{1,0:T(8,128)S(1)} fusion(bf16[8,2,512,256]{2,3,1,0:T(8,128)(2,1)S(1)} %copy-done.5, bf16[8,2,512,256]{2,3,1,0:T(8,128)(2,1)} %copy.170, pred[]{:T(512)} %bitcast.48, bf16[8,1,2,256,256]{4,3,2,0,1:T(8,128)(2,1)} %get-tuple-element.130, bf16[8,1,2,256,256]{4,3,2,0,1:T(8,128)(2,1)} %get-tuple-element.129), kind=kOutput, calls=%fused_computation.53 | convolution fusion | flops 2157965312 | bytes 12599297 | tf_op jit(solution)/shard_map/tdcrq,tckq->tdkr/dot_general | solution.py:68
  322.4 4.6 %pad_maximum_fusion.1 = bf16[2,8,2,256,256]{4,3,2,1,0:T(8,128)(2,1)} fusion(bf16[1,8,2,256,256]{4,3,2,1,0:T(8,128)(2,1)} %bitcast.180, bf16[1,8,2,256,256]{4,3,2,1,0:T(8,128)(2,1)} %bitcast.179), kind=kLoop, calls=%fused_computation.63 | loop fusion | flops 2097152 | bytes 8388608 | tf_op jit(solution)/shard_map/stack | solution.py:153
  327.0 90.5 %reduce-scatter.4.cloned.1.call-done = f32[32,8]{1,0:T(8,128)} async-done(((f32[512,8]{1,0:T(8,128)}), f32[32,8]{1,0:T(8,128)}) %reduce-scatter.4.cloned.1.call-update) | async-done | bytes 1040
  (63 shorter events, 13.5 us)
Async XLA Ops:
  7.2 4.5 %copy-start.15 = (s32[8,32]{1,0:T(8,128)S(1)}, s32[8,32]{1,0:T(8,128)}, u32[]{:S(2)}) copy-start(s32[8,32]{1,0:T(8,128)} %param.23) | copy-start | bytes 3076
  7.2 187.5 %all-gather.3.cloned.1.call-start = ((), (), s32[]{:S(2)}) async-start(), calls=%async_computation.1 | async-start | bytes 35651584 | tf_op jit(solution)/shard_map/all_gather | solution.py:132
  21.1 2.6 copy-start.17
  21.2 2.6 copy-start.18
  21.2 5.9 %copy-start.16 = (s32[32]{0:T(128)S(1)}, s32[32]{0:T(128)}, u32[]{:S(2)}) copy-start(s32[32]{0:T(128)} %constant.62.clone) | copy-start | bytes 388
  21.2 32.1 %copy-start.14 = (s32[8,2048]{1,0:T(8,128)S(1)}, s32[8,2048]{1,0:T(8,128)}, u32[]{:S(2)}) copy-start(s32[8,2048]{1,0:T(8,128)} %param.24) | copy-start | bytes 196612
  23.7 393.8 %reduce-scatter.4.cloned.1.call-start = ((), (), s32[]{:S(2)}) async-start(), calls=%async_computation.2 | async-start | bytes 278528
  229.8 2.7 copy-start.9
  248.0 4.3 %copy-start = (bf16[8,2,512,256]{2,3,1,0:T(8,128)(2,1)S(1)}, bf16[8,2,512,256]{2,3,1,0:T(8,128)(2,1)}, u32[]{:S(2)}) copy-start(bf16[8,2,512,256]{2,3,1,0:T(8,128)(2,1)} %copy.168) | copy-start | bytes 12582916
  248.0 5.6 %copy-start.6 = (bf16[8,2,512,256]{2,3,1,0:T(8,128)(2,1)S(1)}, bf16[8,2,512,256]{2,3,1,0:T(8,128)(2,1)}, u32[]{:S(2)}) copy-start(bf16[8,2,512,256]{2,3,1,0:T(8,128)(2,1)} %copy.167) | copy-start | bytes 12582916
  262.0 3.3 copy-start.7
  282.2 4.3 %copy-start.4 = (bf16[8,2,512,256]{2,3,1,0:T(8,128)(2,1)S(1)}, bf16[8,2,512,256]{2,3,1,0:T(8,128)(2,1)}, u32[]{:S(2)}) copy-start(bf16[8,2,512,256]{2,3,1,0:T(8,128)(2,1)} %copy.169) | copy-start | bytes 12582916
  282.2 5.6 %copy-start.8 = (bf16[8,2,512,256]{2,3,1,0:T(8,128)(2,1)S(1)}, bf16[8,2,512,256]{2,3,1,0:T(8,128)(2,1)}, u32[]{:S(2)}) copy-start(bf16[8,2,512,256]{2,3,1,0:T(8,128)(2,1)} %get-tuple-element.141) | copy-start | bytes 12582916
  298.4 1.2 copy-start.10
  298.4 5.8 %copy-start.1 = (bf16[8,2,512,256]{2,3,1,0:T(8,128)(2,1)S(1)}, bf16[8,2,512,256]{2,3,1,0:T(8,128)(2,1)}, u32[]{:S(2)}) copy-start(bf16[8,2,512,256]{2,3,1,0:T(8,128)(2,1)} %copy.168) | copy-start | bytes 12582916
  304.2 6.5 %copy-start.11 = (bf16[8,1,256,256]{3,2,1,0:T(8,128)(2,1)S(1)}, bf16[8,1,256,256]{3,2,1,0:T(8,128)(2,1)}, u32[]{:S(2)}) copy-start(bf16[8,1,256,256]{3,2,1,0:T(8,128)(2,1)} %get-tuple-element.124) | copy-start | bytes 3145732
  304.2 6.5 %copy-start.12 = (bf16[8,1,256,256]{3,2,1,0:T(8,128)(2,1)S(1)}, bf16[8,1,256,256]{3,2,1,0:T(8,128)(2,1)}, u32[]{:S(2)}) copy-start(bf16[8,1,256,256]{3,2,1,0:T(8,128)(2,1)} %get-tuple-element.125) | copy-start | bytes 3145732
  310.6 4.2 copy-start.5
Sparse Core Ops, SparseCore 0:
  23.8 170.8 all-gather.2
  322.5 94.9 reduce-scatter.3
where the time goes:
time: 427 us; the launch traced here: 426 us
  waiting for transfers between devices  229 us (54%)
  local copies, waits for them, and re-layouts  72.1 us (17%)
  other arithmetic  52 us (12%)
  matrix products  30 us (7%)
  blocking collectives  23.9 us (6%)
  between operations  18.3 us (4%)
    all_gather x1, waiting for transfers between devices, per_device(): lax.all_gather(owned, 'tile', axis=2, tiled=True)  139 us
    unnamed x3, waiting for transfers between devices  90.5 us
    unnamed x39, local copies, waits for them, and re-layouts  38.4 us
    all_gather x1, blocking collectives, per_device(): lax.all_gather(brightness, 'tile', axis=1, tiled=True)  23.9 us
    dot_general x2, matrix products, predict(): jnp.einsum('tdckr,tckq->tdrq', stacked, cols_f, preferred_element_type=jn...  17.2 us
    dot_general x2, matrix products, pull_back(): jnp.einsum('tdcrq,tckq->tdkr', rstack, cols_f, preferred_element_type=jnp...  12.9 us
    dynamic_slice x1, local copies, waits for them, and re-layouts, per_device(): block_one = lax.dynamic_slice_in_dim(gathered, start_one, span, 3)  12.4 us
    cond x2, local copies, waits for them, and re-layouts, unit_work(): lax.cond(diag_tile, lambda: predict(block_two, block_two, bright_all), la...  10.8 us
  transfers between devices with their start and end apart: 2, of which 2 were waited for; matrix products, arithmetic and copies ran while one was open for 2% of the time, Pallas kernels for 0%

commit v1 on v0

--- a/solution.py
+++ b/solution.py
@@ -113,6 +113,32 @@
 def per_device(
     visibility, station_beam, antenna_uvw, source_dirs, source_flux, visible_list, antenna_flags
 ):
+
+    def direct_group(frame_in):
+        frame_out = lax.axis_size("tile")
+        carry = lax.axis_index("tile")
+        f_now, piece_next, inter = (frame_out, carry, frame_in.shape[2])
+        pool = [nth * f_now if k0 == 2 else nth for k0, nth in enumerate(frame_in.shape)]
+        v_next = jnp.zeros(pool, frame_in.dtype)
+        p_next = lax.dynamic_update_slice_in_dim(v_next, frame_in, piece_next * inter, axis=2)
+        oldest = shaped = frame_in
+        for rr in range(1, f_now // 2 + 1):
+            oldest = lax.ppermute(
+                oldest,
+                axis_name="tile",
+                perm=list(map(lambda k0: (k0, (k0 + 1) % f_now), range(f_now))),
+            )
+            p_next = lax.dynamic_update_slice_in_dim(
+                p_next, oldest, (piece_next - rr) % f_now * inter, axis=2
+            )
+            if 2 * rr < f_now:
+                then = map(lambda k0: (k0, (k0 - 1) % f_now), range(f_now))
+                shaped = lax.ppermute(shaped, axis_name="tile", perm=list(then))
+                p_next = lax.dynamic_update_slice_in_dim(
+                    p_next, shaped, (piece_next + rr) % f_now * inter, axis=2
+                )
+        return p_next
+
     tile_count = lax.axis_size("tile")
     units_dev = visibility.shape[0]
     span = visibility.shape[4]
@@ -129,7 +155,7 @@
         station_beam, antenna_uvw, source_dirs, source_flux, visible_list
     )
     gathered, bright_all = (
-        lax.all_gather(owned, "tile", axis=2, tiled=True),
+        direct_group(owned),
         lax.all_gather(brightness, "tile", axis=1, tiled=True),
     )
     residuals = []

time: 427 us -> 2150 us (5.04); the launches traced: 426 us -> 2110 us
  local copies, waits for them, and re-layouts: 72.1 us -> 1560 us
  starting transfers between devices: 0.08 us -> 280 us
  waiting for transfers between devices: 229 us -> 141 us
    dynamic_update_slice x0 -> x16, local copies, waits for them, and re-layouts: none -> 1410 us  [the longest x8 701 us: direct_group(): lax.dynamic_update_slice_in_dim(p_next, oldest, (piece_next - rr) % f_now...]
    ppermute x0 -> x15, starting transfers between devices: none -> 279 us  [the longest x8 274 us: direct_group(): lax.ppermute(oldest, axis_name='tile', perm=list(map(lambda k0: (k0, (k0...]
    all_gather x1 -> x0, waiting for transfers between devices: 139 us -> none  [per_device(): lax.all_gather(owned, 'tile', axis=2, tiled=True)]
    ppermute x0 -> x15, local copies, waits for them, and re-layouts: none -> 95.8 us  [the longest x8 50.8 us: direct_group(): lax.ppermute(oldest, axis_name='tile', perm=list(map(lambda k0: (k0, (k0...]
    ppermute x0 -> x15, waiting for transfers between devices: none -> 50.5 us  [the longest x8 50.5 us: direct_group(): lax.ppermute(oldest, axis_name='tile', perm=list(map(lambda k0: (k0, (k0...]
    unnamed x39 -> x83, local copies, waits for them, and re-layouts: 38.4 us -> 10.3 us
    unnamed x3 -> x2, waiting for transfers between devices: 90.5 us -> 90.8 us
  transfers between devices with their start and end apart: 2 -> 16, of which waited for: 2 -> 8; matrix products, arithmetic and copies ran while one was open for 2% -> 68% of each run, Pallas kernels for 0% -> 0%
where the time goes in v1:
time: 2150 us; the launch traced here: 2110 us
  local copies, waits for them, and re-layouts  1560 us (73%)
  starting transfers between devices  280 us (13%)
  waiting for transfers between devices  141 us (7%)
  other arithmetic  53.1 us (2%)
  matrix products  33.3 us (2%)
  blocking collectives  26.6 us (1%)
    dynamic_update_slice x8, local copies, waits for them, and re-layouts, direct_group(): lax.dynamic_update_slice_in_dim(p_next, oldest, (piece_next - rr) % f_now...  701 us
    dynamic_update_slice x7, local copies, waits for them, and re-layouts, direct_group(): lax.dynamic_update_slice_in_dim(p_next, shaped, (piece_next + rr) % f_now...  629 us
    ppermute x8, starting transfers between devices, direct_group(): lax.ppermute(oldest, axis_name='tile', perm=list(map(lambda k0: (k0, (k0...  274 us
    unnamed x2, waiting for transfers between devices  90.8 us
    dynamic_update_slice x1, local copies, waits for them, and re-layouts, direct_group(): lax.dynamic_update_slice_in_dim(v_next, frame_in, piece_next * inter, axi...  78.6 us
    ppermute x8, local copies, waits for them, and re-layouts, direct_group(): lax.ppermute(oldest, axis_name='tile', perm=list(map(lambda k0: (k0, (k0...  50.8 us
    ppermute x8, waiting for transfers between devices, direct_group(): lax.ppermute(oldest, axis_name='tile', perm=list(map(lambda k0: (k0, (k0...  50.5 us
    ppermute x7, local copies, waits for them, and re-layouts, direct_group(): shaped = lax.ppermute(shaped, axis_name='tile', perm=list(then))  45 us
  transfers between devices with their start and end apart: 16, of which 8 were waited for; matrix products, arithmetic and copies ran while one was open for 68% of the time, Pallas kernels for 0%

profile of v1, /device:TPU:0, one launch (start us, length us, event | category | flops | bytes accessed | tf_op | source)
XLA Modules:
  0.0 2111.4 jit_solution(16064458773416065701)
XLA Ops:
  12.0 8.9 add_convert_fusion
  26.7 23.8 %collective-permute-done = bf16[8,2,32,2048]{3,2,1,0:T(8,128)(2,1)S(1)} collective-permute-done((bf16[8,2,32,2048]{3,2,1,0:T(8,128)(2,1)S(1)}, bf16[8,2,32,2048]{3,2,1,0:T(8,128)(2,1)S(1)}, u32[]{:S(2)}, u32[]{:S(2)}) %collective-permute-start) | collective-permute-done | bytes 2097184 | tf_op jit(solution)/shard_map/ppermute | solution.py:126
  50.5 19.3 collective-permute-start.2
  78.8 38.9 %collective-permute-start.4 = (bf16[8,2,32,2048]{3,2,1,0:T(8,128)(2,1)S(1)}, bf16[8,2,32,2048]{3,2,1,0:T(8,128)(2,1)S(1)}, u32[]{:S(2)}, u32[]{:S(2)}) collective-permute-start(bf16[8,2,32,2048]{3,2,1,0:T(8,128)(2,1)S(1)} %collective-permute-done.2), channel_id=1, source_target_pairs={{0,1},{1,2},{2,3},{3,4},{4,5},{5,6},{6,7},{7,8},{8,9},{9,10},{10,1... | collective-permute-start | bytes 6291464 | tf_op jit(solution)/shard_map/ppermute | solution.py:126
  121.9 43.0 %collective-permute-start.6 = (bf16[8,2,32,2048]{3,2,1,0:T(8,128)(2,1)S(1)}, bf16[8,2,32,2048]{3,2,1,0:T(8,128)(2,1)S(1)}, u32[]{:S(2)}, u32[]{:S(2)}) collective-permute-start(bf16[8,2,32,2048]{3,2,1,0:T(8,128)(2,1)S(1)} %collective-permute-done.4), channel_id=1, source_target_pairs={{0,1},{1,2},{2,3},{3,4},{4,5},{5,6},{6,7},{7,8},{8,9},{9,10},{10,1... | collective-permute-start | bytes 6291464 | tf_op jit(solution)/shard_map/ppermute | solution.py:126
  168.7 43.4 %collective-permute-start.8 = (bf16[8,2,32,2048]{3,2,1,0:T(8,128)(2,1)S(1)}, bf16[8,2,32,2048]{3,2,1,0:T(8,128)(2,1)S(1)}, u32[]{:S(2)}, u32[]{:S(2)}) collective-permute-start(bf16[8,2,32,2048]{3,2,1,0:T(8,128)(2,1)S(1)} %collective-permute-done.6), channel_id=1, source_target_pairs={{0,1},{1,2},{2,3},{3,4},{4,5},{5,6},{6,7},{7,8},{8,9},{9,10},{10,1... | collective-permute-start | bytes 6291464 | tf_op jit(solution)/shard_map/ppermute | solution.py:126
  215.9 42.7 %collective-permute-start.10 = (bf16[8,2,32,2048]{3,2,1,0:T(8,128)(2,1)S(1)}, bf16[8,2,32,2048]{3,2,1,0:T(8,128)(2,1)S(1)}, u32[]{:S(2)}, u32[]{:S(2)}) collective-permute-start(bf16[8,2,32,2048]{3,2,1,0:T(8,128)(2,1)S(1)} %collective-permute-done.8), channel_id=1, source_target_pairs={{0,1},{1,2},{2,3},{3,4},{4,5},{5,6},{6,7},{7,8},{8,9},{9,10},{10,1... | collective-permute-start | bytes 6291464 | tf_op jit(solution)/shard_map/ppermute | solution.py:126
  262.4 42.8 %collective-permute-start.12 = (bf16[8,2,32,2048]{3,2,1,0:T(8,128)(2,1)S(1)}, bf16[8,2,32,2048]{3,2,1,0:T(8,128)(2,1)}, u32[]{:S(2)}, u32[]{:S(2)}) collective-permute-start(bf16[8,2,32,2048]{3,2,1,0:T(8,128)(2,1)S(1)} %collective-permute-done.10), channel_id=1, source_target_pairs={{0,1},{1,2},{2,3},{3,4},{4,5},{5,6},{6,7},{7,8},{8,9},{9,10},{10,1... | collective-permute-start | bytes 6291464 | tf_op jit(solution)/shard_map/ppermute | solution.py:126
  309.2 43.5 %collective-permute-start.14 = (bf16[8,2,32,2048]{3,2,1,0:T(8,128)(2,1)}, bf16[8,2,32,2048]{3,2,1,0:T(8,128)(2,1)}, u32[]{:S(2)}, u32[]{:S(2)}) collective-permute-start(bf16[8,2,32,2048]{3,2,1,0:T(8,128)(2,1)} %collective-permute-done.12), channel_id=1, source_target_pairs={{0,1},{1,2},{2,3},{3,4},{4,5},{5,6},{6,7},{7,8},{8,9},{9,10},{10,1... | collective-permute-start | bytes 6291464 | tf_op jit(solution)/shard_map/ppermute | solution.py:126
  363.6 26.6 %all-gather = bf16[16,32,8]{1,2,0:T(8,128)(2,1)S(1)} all-gather(bf16[1,32,8]{1,2,0:T(8,128)(2,1)S(1)} %bitcast.185), channel_id=1, replica_groups=mesh['grp'=2,'tile'=16] {'tile'}, dimensions={0}, use_global_device_ids=true | all-gather | bytes 8704 | tf_op jit(solution)/shard_map/all_gather | solution.py:159
  390.6 10.9 broadcast_in_dim.106
  401.5 78.6 %dynamic_update_slice.48 = bf16[8,2,512,2048]{2,3,1,0:T(8,128)(2,1)} dynamic-update-slice(bf16[8,2,512,2048]{2,3,1,0:T(8,128)(2,1)} %broadcast_in_dim.106, bf16[8,2,32,2048]{2,3,1,0:T(8,128)(2,1)} %copy.126, s32[]{:T(128)} %constant.129.clone.1, s32[]{:T(128)} %constant.129.clone.1, s32[]{:T(128)S(6)} %select_n.210, s32[]{:T(128)} %constant.129.clone.1) | dynamic-update-slice | bytes 4194308 | tf_op jit(solution)/shard_map/dynamic_update_slice | solution.py:123
  490.1 90.2 %dynamic_update_slice.49 = bf16[8,2,512,2048]{2,3,1,0:T(8,128)(2,1)} dynamic-update-slice(bf16[8,2,512,2048]{2,3,1,0:T(8,128)(2,1)} %dynamic_update_slice.48, bf16[8,2,32,2048]{2,3,1,0:T(8,128)(2,1)} %copy.127, s32[]{:T(128)} %constant.129.clone.1, s32[]{:T(128)} %constant.129.clone.1, s32[]{:T(128)S(6)} %select_n.212, s32[]{:T(128)} %constant.129.clone.1) | dynamic-update-slice | bytes 4194308 | tf_op jit(solution)/shard_map/dynamic_update_slice | solution.py:131
  586.2 91.8 %dynamic_update_slice.50 = bf16[8,2,512,2048]{2,3,1,0:T(8,128)(2,1)} dynamic-update-slice(bf16[8,2,512,2048]{2,3,1,0:T(8,128)(2,1)} %dynamic_update_slice.49, bf16[8,2,32,2048]{2,3,1,0:T(8,128)(2,1)} %copy.128, s32[]{:T(128)} %constant.129.clone.1, s32[]{:T(128)} %constant.129.clone.1, s32[]{:T(128)S(6)} %select_n.214, s32[]{:T(128)} %constant.129.clone.1) | dynamic-update-slice | bytes 4194308 | tf_op jit(solution)/shard_map/dynamic_update_slice | solution.py:137
  683.9 90.2 %dynamic_update_slice.51 = bf16[8,2,512,2048]{2,3,1,0:T(8,128)(2,1)} dynamic-update-slice(bf16[8,2,512,2048]{2,3,1,0:T(8,128)(2,1)} %dynamic_update_slice.50, bf16[8,2,32,2048]{2,3,1,0:T(8,128)(2,1)} %copy.129, s32[]{:T(128)} %constant.129.clone.1, s32[]{:T(128)} %constant.129.clone.1, s32[]{:T(128)S(6)} %select_n.216, s32[]{:T(128)} %constant.129.clone.1) | dynamic-update-slice | bytes 4194308 | tf_op jit(solution)/shard_map/dynamic_update_slice | solution.py:131
  780.0 91.8 %dynamic_update_slice.52 = bf16[8,2,512,2048]{2,3,1,0:T(8,128)(2,1)} dynamic-update-slice(bf16[8,2,512,2048]{2,3,1,0:T(8,128)(2,1)} %dynamic_update_slice.51, bf16[8,2,32,2048]{2,3,1,0:T(8,128)(2,1)} %copy.130, s32[]{:T(128)} %constant.129.clone.1, s32[]{:T(128)} %constant.129.clone.1, s32[]{:T(128)S(6)} %select_n.218, s32[]{:T(128)} %constant.129.clone.1) | dynamic-update-slice | bytes 4194308 | tf_op jit(solution)/shard_map/dynamic_update_slice | solution.py:137
  877.7 90.2 %dynamic_update_slice.53 = bf16[8,2,512,2048]{2,3,1,0:T(8,128)(2,1)} dynamic-update-slice(bf16[8,2,512,2048]{2,3,1,0:T(8,128)(2,1)} %dynamic_update_slice.52, bf16[8,2,32,2048]{2,3,1,0:T(8,128)(2,1)} %copy.131, s32[]{:T(128)} %constant.129.clone.1, s32[]{:T(128)} %constant.129.clone.1, s32[]{:T(128)S(6)} %select_n.220, s32[]{:T(128)} %constant.129.clone.1) | dynamic-update-slice | bytes 4194308 | tf_op jit(solution)/shard_map/dynamic_update_slice | solution.py:131
  973.8 91.8 %dynamic_update_slice.54 = bf16[8,2,512,2048]{2,3,1,0:T(8,128)(2,1)} dynamic-update-slice(bf16[8,2,512,2048]{2,3,1,0:T(8,128)(2,1)} %dynamic_update_slice.53, bf16[8,2,32,2048]{2,3,1,0:T(8,128)(2,1)} %copy.132, s32[]{:T(128)} %constant.129.clone.1, s32[]{:T(128)} %constant.129.clone.1, s32[]{:T(128)S(6)} %select_n.222, s32[]{:T(128)} %constant.129.clone.1) | dynamic-update-slice | bytes 4194308 | tf_op jit(solution)/shard_map/dynamic_update_slice | solution.py:137
  1071.5 76.7 %dynamic_update_slice.55 = bf16[8,2,512,2048]{2,3,1,0:T(8,128)(2,1)} dynamic-update-slice(bf16[8,2,512,2048]{2,3,1,0:T(8,128)(2,1)} %dynamic_update_slice.54, bf16[8,2,32,2048]{2,3,1,0:T(8,128)(2,1)} %copy.133, s32[]{:T(128)} %constant.129.clone.1, s32[]{:T(128)} %constant.129.clone.1, s32[]{:T(128)S(6)} %select_n.224, s32[]{:T(128)} %constant.129.clone.1) | dynamic-update-slice | bytes 4194308 | tf_op jit(solution)/shard_map/dynamic_update_slice | solution.py:131
  1154.2 78.6 %dynamic_update_slice.56 = bf16[8,2,512,2048]{2,3,1,0:T(8,128)(2,1)} dynamic-update-slice(bf16[8,2,512,2048]{2,3,1,0:T(8,128)(2,1)} %dynamic_update_slice.55, bf16[8,2,32,2048]{2,3,1,0:T(8,128)(2,1)} %copy.134, s32[]{:T(128)} %constant.129.clone.1, s32[]{:T(128)} %constant.129.clone.1, s32[]{:T(128)S(6)} %select_n.226, s32[]{:T(128)} %constant.129.clone.1) | dynamic-update-slice | bytes 4194308 | tf_op jit(solution)/shard_map/dynamic_update_slice | solution.py:137
  1238.7 91.8 %dynamic_update_slice.57 = bf16[8,2,512,2048]{2,3,1,0:T(8,128)(2,1)} dynamic-update-slice(bf16[8,2,512,2048]{2,3,1,0:T(8,128)(2,1)} %dynamic_update_slice.56, bf16[8,2,32,2048]{2,3,1,0:T(8,128)(2,1)} %copy.135, s32[]{:T(128)} %constant.129.clone.1, s32[]{:T(128)} %constant.129.clone.1, s32[]{:T(128)S(6)} %select_n.228, s32[]{:T(128)} %constant.129.clone.1) | dynamic-update-slice | bytes 4194308 | tf_op jit(solution)/shard_map/dynamic_update_slice | solution.py:131
  1336.4 91.8 %dynamic_update_slice.58 = bf16[8,2,512,2048]{2,3,1,0:T(8,128)(2,1)} dynamic-update-slice(bf16[8,2,512,2048]{2,3,1,0:T(8,128)(2,1)} %dynamic_update_slice.57, bf16[8,2,32,2048]{2,3,1,0:T(8,128)(2,1)} %copy.136, s32[]{:T(128)} %constant.129.clone.1, s32[]{:T(128)} %constant.129.clone.1, s32[]{:T(128)S(6)} %select_n.230, s32[]{:T(128)} %constant.129.clone.1) | dynamic-update-slice | bytes 4194308 | tf_op jit(solution)/shard_map/dynamic_update_slice | solution.py:137
  1434.1 91.7 %dynamic_update_slice.59 = bf16[8,2,512,2048]{2,3,1,0:T(8,128)(2,1)} dynamic-update-slice(bf16[8,2,512,2048]{2,3,1,0:T(8,128)(2,1)} %dynamic_update_slice.58, bf16[8,2,32,2048]{2,3,1,0:T(8,128)(2,1)} %copy.137, s32[]{:T(128)} %constant.129.clone.1, s32[]{:T(128)} %constant.129.clone.1, s32[]{:T(128)S(6)} %select_n.232, s32[]{:T(128)} %constant.129.clone.1) | dynamic-update-slice | bytes 4194308 | tf_op jit(solution)/shard_map/dynamic_update_slice | solution.py:131
  1533.6 91.7 %dynamic_update_slice.60 = bf16[8,2,512,2048]{2,3,1,0:T(8,128)(2,1)} dynamic-update-slice(bf16[8,2,512,2048]{2,3,1,0:T(8,128)(2,1)} %dynamic_update_slice.59, bf16[8,2,32,2048]{2,3,1,0:T(8,128)(2,1)} %copy.138, s32[]{:T(128)} %constant.129.clone.1, s32[]{:T(128)} %constant.129.clone.1, s32[]{:T(128)S(6)} %select_n.234, s32[]{:T(128)} %constant.129.clone.1) | dynamic-update-slice | bytes 4194308 | tf_op jit(solution)/shard_map/dynamic_update_slice | solution.py:137
  1633.0 91.7 %dynamic_update_slice.61 = bf16[8,2,512,2048]{2,3,1,0:T(8,128)(2,1)} dynamic-update-slice(bf16[8,2,512,2048]{2,3,1,0:T(8,128)(2,1)} %dynamic_update_slice.60, bf16[8,2,32,2048]{2,3,1,0:T(8,128)(2,1)} %copy.139, s32[]{:T(128)} %constant.129.clone.1, s32[]{:T(128)} %constant.129.clone.1, s32[]{:T(128)S(6)} %select_n.236, s32[]{:T(128)} %constant.129.clone.1) | dynamic-update-slice | bytes 4194308 | tf_op jit(solution)/shard_map/dynamic_update_slice | solution.py:131
  1724.7 7.8 copy.140
  1732.5 91.7 %dynamic_update_slice.62 = bf16[8,2,512,2048]{2,3,1,0:T(8,128)(2,1)} dynamic-update-slice(bf16[8,2,512,2048]{2,3,1,0:T(8,128)(2,1)} %dynamic_update_slice.61, bf16[8,2,32,2048]{2,3,1,0:T(8,128)(2,1)} %copy.140, s32[]{:T(128)} %constant.129.clone.1, s32[]{:T(128)} %constant.129.clone.1, s32[]{:T(128)S(6)} %select_n.238, s32[]{:T(128)} %constant.129.clone.1) | dynamic-update-slice | bytes 4194308 | tf_op jit(solution)/shard_map/dynamic_update_slice | solution.py:137
  1831.9 78.7 %dynamic_update_slice.63 = bf16[8,2,512,2048]{2,3,1,0:T(8,128)(2,1)} dynamic-update-slice(bf16[8,2,512,2048]{2,3,1,0:T(8,128)(2,1)} %dynamic_update_slice.62, bf16[8,2,32,2048]{2,3,1,0:T(8,128)(2,1)} %copy.141, s32[]{:T(128)} %constant.129.clone.1, s32[]{:T(128)} %constant.129.clone.1, s32[]{:T(128)S(6)} %select_n.240, s32[]{:T(128)} %constant.129.clone.1) | dynamic-update-slice | bytes 4194308 | tf_op jit(solution)/shard_map/dynamic_update_slice | solution.py:131
  1910.6 7.8 constant_dynamic-slice_fusion.3
  1942.1 9.1 broadcast_select_fusion.3
  1969.7 9.0 broadcast_select_fusion.2
  2012.1 90.8 %reduce-scatter.4.cloned.1.call-done = f32[32,8]{1,0:T(8,128)} async-done(((f32[512,8]{1,0:T(8,128)}), f32[32,8]{1,0:T(8,128)}) %reduce-scatter.4.cloned.1.call-update) | async-done | bytes 1040
  (166 shorter events, 220.2 us)
Async XLA Ops:
  7.2 2095.7 %reduce-scatter.4.cloned.1.call-start = ((), (), s32[]{:S(2)}) async-start(), calls=%async_computation.1 | async-start | bytes 278528
  21.1 29.3 %collective-permute-start = (bf16[8,2,32,2048]{3,2,1,0:T(8,128)(2,1)S(1)}, bf16[8,2,32,2048]{3,2,1,0:T(8,128)(2,1)S(1)}, u32[]{:S(2)}, u32[]{:S(2)}) collective-permute-start(bf16[8,2,32,2048]{3,2,1,0:T(8,128)(2,1)S(1)} %pad_maximum_fusion.4), channel_id=1, source_target_pairs={{0,1},{1,2},{2,3},{3,4},{4,5},{5,6},{6,7},{7,8},{8,9},{9,10},{10,1... | collective-permute-start | bytes 6291464 | tf_op jit(solution)/shard_map/ppermute | solution.py:126
  21.7 48.1 %collective-permute-start.1 = (bf16[8,2,32,2048]{3,2,1,0:T(8,128)(2,1)S(1)}, bf16[8,2,32,2048]{3,2,1,0:T(8,128)(2,1)S(1)}, u32[]{:S(2)}, u32[]{:S(2)}) collective-permute-start(bf16[8,2,32,2048]{3,2,1,0:T(8,128)(2,1)S(1)} %pad_maximum_fusion.4), channel_id=1, source_target_pairs={{0,15},{1,0},{2,1},{3,2},{4,3},{5,4},{6,5},{7,6},{8,7},{9,8},{10,9... | collective-permute-start | bytes 6291464 | tf_op jit(solution)/shard_map/ppermute | solution.py:136
  50.5 71.4 %copy-start.21 = (bf16[8,2,32,2048]{3,2,1,0:T(8,128)(2,1)}, bf16[8,2,32,2048]{3,2,1,0:T(8,128)(2,1)S(1)}, u32[]{:S(2)}) copy-start(bf16[8,2,32,2048]{3,2,1,0:T(8,128)(2,1)S(1)} %collective-permute-done) | copy-start | bytes 6291460
  50.5 28.3 %collective-permute-start.2 = (bf16[8,2,32,2048]{3,2,1,0:T(8,128)(2,1)S(1)}, bf16[8,2,32,2048]{3,2,1,0:T(8,128)(2,1)S(1)}, u32[]{:S(2)}, u32[]{:S(2)}) collective-permute-start(bf16[8,2,32,2048]{3,2,1,0:T(8,128)(2,1)S(1)} %collective-permute-done), channel_id=1, source_target_pairs={{0,1},{1,2},{2,3},{3,4},{4,5},{5,6},{6,7},{7,8},{8,9},{9,10},{10,1... | collective-permute-start | bytes 6291464 | tf_op jit(solution)/shard_map/ppermute | solution.py:126
  71.1 46.6 %collective-permute-start.3 = (bf16[8,2,32,2048]{3,2,1,0:T(8,128)(2,1)S(1)}, bf16[8,2,32,2048]{3,2,1,0:T(8,128)(2,1)S(1)}, u32[]{:S(2)}, u32[]{:S(2)}) collective-permute-start(bf16[8,2,32,2048]{3,2,1,0:T(8,128)(2,1)S(1)} %collective-permute-done.1), channel_id=1, source_target_pairs={{0,15},{1,0},{2,1},{3,2},{4,3},{5,4},{6,5},{7,6},{8,7},{9,8},{10,9... | collective-permute-start | bytes 6291464 | tf_op jit(solution)/shard_map/ppermute | solution.py:136
  78.8 43.1 %collective-permute-start.4 = (bf16[8,2,32,2048]{3,2,1,0:T(8,128)(2,1)S(1)}, bf16[8,2,32,2048]{3,2,1,0:T(8,128)(2,1)S(1)}, u32[]{:S(2)}, u32[]{:S(2)}) collective-permute-start(bf16[8,2,32,2048]{3,2,1,0:T(8,128)(2,1)S(1)} %collective-permute-done.2), channel_id=1, source_target_pairs={{0,1},{1,2},{2,3},{3,4},{4,5},{5,6},{6,7},{7,8},{8,9},{9,10},{10,1... | collective-permute-start | bytes 6291464 | tf_op jit(solution)/shard_map/ppermute | solution.py:126
  117.7 47.2 %copy-start.23 = (bf16[8,2,32,2048]{3,2,1,0:T(8,128)(2,1)}, bf16[8,2,32,2048]{3,2,1,0:T(8,128)(2,1)S(1)}, u32[]{:S(2)}) copy-start(bf16[8,2,32,2048]{3,2,1,0:T(8,128)(2,1)S(1)} %collective-permute-done.3) | copy-start | bytes 6291460
  117.7 47.2 %collective-permute-start.5 = (bf16[8,2,32,2048]{3,2,1,0:T(8,128)(2,1)S(1)}, bf16[8,2,32,2048]{3,2,1,0:T(8,128)(2,1)S(1)}, u32[]{:S(2)}, u32[]{:S(2)}) collective-permute-start(bf16[8,2,32,2048]{3,2,1,0:T(8,128)(2,1)S(1)} %collective-permute-done.3), channel_id=1, source_target_pairs={{0,15},{1,0},{2,1},{3,2},{4,3},{5,4},{6,5},{7,6},{8,7},{9,8},{10,9... | collective-permute-start | bytes 6291464 | tf_op jit(solution)/shard_map/ppermute | solution.py:136
  121.9 43.0 %copy-start.25 = (bf16[8,2,32,2048]{3,2,1,0:T(8,128)(2,1)}, bf16[8,2,32,2048]{3,2,1,0:T(8,128)(2,1)S(1)}, u32[]{:S(2)}) copy-start(bf16[8,2,32,2048]{3,2,1,0:T(8,128)(2,1)S(1)} %collective-permute-done.4) | copy-start | bytes 6291460
  121.9 46.8 %collective-permute-start.6 = (bf16[8,2,32,2048]{3,2,1,0:T(8,128)(2,1)S(1)}, bf16[8,2,32,2048]{3,2,1,0:T(8,128)(2,1)S(1)}, u32[]{:S(2)}, u32[]{:S(2)}) collective-permute-start(bf16[8,2,32,2048]{3,2,1,0:T(8,128)(2,1)S(1)} %collective-permute-done.4), channel_id=1, source_target_pairs={{0,1},{1,2},{2,3},{3,4},{4,5},{5,6},{6,7},{7,8},{8,9},{9,10},{10,1... | collective-permute-start | bytes 6291464 | tf_op jit(solution)/shard_map/ppermute | solution.py:126
  164.9 47.2 %collective-permute-start.7 = (bf16[8,2,32,2048]{3,2,1,0:T(8,128)(2,1)S(1)}, bf16[8,2,32,2048]{3,2,1,0:T(8,128)(2,1)S(1)}, u32[]{:S(2)}, u32[]{:S(2)}) collective-permute-start(bf16[8,2,32,2048]{3,2,1,0:T(8,128)(2,1)S(1)} %collective-permute-done.5), channel_id=1, source_target_pairs={{0,15},{1,0},{2,1},{3,2},{4,3},{5,4},{6,5},{7,6},{8,7},{9,8},{10,9... | collective-permute-start | bytes 6291464 | tf_op jit(solution)/shard_map/ppermute | solution.py:136
  168.7 43.5 %copy-start.29 = (bf16[8,2,32,2048]{3,2,1,0:T(8,128)(2,1)}, bf16[8,2,32,2048]{3,2,1,0:T(8,128)(2,1)S(1)}, u32[]{:S(2)}) copy-start(bf16[8,2,32,2048]{3,2,1,0:T(8,128)(2,1)S(1)} %collective-permute-done.6) | copy-start | bytes 6291460
  168.7 47.2 %collective-permute-start.8 = (bf16[8,2,32,2048]{3,2,1,0:T(8,128)(2,1)S(1)}, bf16[8,2,32,2048]{3,2,1,0:T(8,128)(2,1)S(1)}, u32[]{:S(2)}, u32[]{:S(2)}) collective-permute-start(bf16[8,2,32,2048]{3,2,1,0:T(8,128)(2,1)S(1)} %collective-permute-done.6), channel_id=1, source_target_pairs={{0,1},{1,2},{2,3},{3,4},{4,5},{5,6},{6,7},{7,8},{8,9},{9,10},{10,1... | collective-permute-start | bytes 6291464 | tf_op jit(solution)/shard_map/ppermute | solution.py:126
  212.2 46.5 %collective-permute-start.9 = (bf16[8,2,32,2048]{3,2,1,0:T(8,128)(2,1)S(1)}, bf16[8,2,32,2048]{3,2,1,0:T(8,128)(2,1)S(1)}, u32[]{:S(2)}, u32[]{:S(2)}) collective-permute-start(bf16[8,2,32,2048]{3,2,1,0:T(8,128)(2,1)S(1)} %collective-permute-done.7), channel_id=1, source_target_pairs={{0,15},{1,0},{2,1},{3,2},{4,3},{5,4},{6,5},{7,6},{8,7},{9,8},{10,9... | collective-permute-start | bytes 6291464 | tf_op jit(solution)/shard_map/ppermute | solution.py:136
  215.9 46.5 %collective-permute-start.10 = (bf16[8,2,32,2048]{3,2,1,0:T(8,128)(2,1)S(1)}, bf16[8,2,32,2048]{3,2,1,0:T(8,128)(2,1)S(1)}, u32[]{:S(2)}, u32[]{:S(2)}) collective-permute-start(bf16[8,2,32,2048]{3,2,1,0:T(8,128)(2,1)S(1)} %collective-permute-done.8), channel_id=1, source_target_pairs={{0,1},{1,2},{2,3},{3,4},{4,5},{5,6},{6,7},{7,8},{8,9},{9,10},{10,1... | collective-permute-start | bytes 6291464 | tf_op jit(solution)/shard_map/ppermute | solution.py:126
  258.6 46.6 %collective-permute-start.11 = (bf16[8,2,32,2048]{3,2,1,0:T(8,128)(2,1)S(1)}, bf16[8,2,32,2048]{3,2,1,0:T(8,128)(2,1)}, u32[]{:S(2)}, u32[]{:S(2)}) collective-permute-start(bf16[8,2,32,2048]{3,2,1,0:T(8,128)(2,1)S(1)} %collective-permute-done.9), channel_id=1, source_target_pairs={{0,15},{1,0},{2,1},{3,2},{4,3},{5,4},{6,5},{7,6},{8,7},{9,8},{10,9... | collective-permute-start | bytes 6291464 | tf_op jit(solution)/shard_map/ppermute | solution.py:136
  262.4 42.8 %copy-start.37 = (bf16[8,2,32,2048]{3,2,1,0:T(8,128)(2,1)}, bf16[8,2,32,2048]{3,2,1,0:T(8,128)(2,1)S(1)}, u32[]{:S(2)}) copy-start(bf16[8,2,32,2048]{3,2,1,0:T(8,128)(2,1)S(1)} %collective-permute-done.10) | copy-start | bytes 6291460
  262.4 46.7 %collective-permute-start.12 = (bf16[8,2,32,2048]{3,2,1,0:T(8,128)(2,1)S(1)}, bf16[8,2,32,2048]{3,2,1,0:T(8,128)(2,1)}, u32[]{:S(2)}, u32[]{:S(2)}) collective-permute-start(bf16[8,2,32,2048]{3,2,1,0:T(8,128)(2,1)S(1)} %collective-permute-done.10), channel_id=1, source_target_pairs={{0,1},{1,2},{2,3},{3,4},{4,5},{5,6},{6,7},{7,8},{8,9},{9,10},{10,1... | collective-permute-start | bytes 6291464 | tf_op jit(solution)/shard_map/ppermute | solution.py:126
  305.2 1419.5 %collective-permute-start.13 = (bf16[8,2,32,2048]{3,2,1,0:T(8,128)(2,1)}, bf16[8,2,32,2048]{3,2,1,0:T(8,128)(2,1)}, u32[]{:S(2)}, u32[]{:S(2)}) collective-permute-start(bf16[8,2,32,2048]{3,2,1,0:T(8,128)(2,1)} %collective-permute-done.11), channel_id=1, source_target_pairs={{0,15},{1,0},{2,1},{3,2},{4,3},{5,4},{6,5},{7,6},{8,7},{9,8},{10,9... | collective-permute-start | bytes 6291464 | tf_op jit(solution)/shard_map/ppermute | solution.py:136
  309.2 1515.0 %collective-permute-start.14 = (bf16[8,2,32,2048]{3,2,1,0:T(8,128)(2,1)}, bf16[8,2,32,2048]{3,2,1,0:T(8,128)(2,1)}, u32[]{:S(2)}, u32[]{:S(2)}) collective-permute-start(bf16[8,2,32,2048]{3,2,1,0:T(8,128)(2,1)} %collective-permute-done.12), channel_id=1, source_target_pairs={{0,1},{1,2},{2,3},{3,4},{4,5},{5,6},{6,7},{7,8},{8,9},{9,10},{10,1... | collective-permute-start | bytes 6291464 | tf_op jit(solution)/shard_map/ppermute | solution.py:126
  401.5 78.6 %copy-start.40 = (s32[8,2048]{1,0:T(8,128)S(1)}, s32[8,2048]{1,0:T(8,128)}, u32[]{:S(2)}) copy-start(s32[8,2048]{1,0:T(8,128)} %param.24) | copy-start | bytes 196612
  490.1 90.2 %copy-start.18 = (bf16[8,2,32,2048]{3,2,1,0:T(8,128)(2,1)S(1)}, bf16[8,2,32,2048]{3,2,1,0:T(8,128)(2,1)}, u32[]{:S(2)}) copy-start(bf16[8,2,32,2048]{3,2,1,0:T(8,128)(2,1)} %copy-done.17) | copy-start | bytes 6291460
  586.2 91.8 %copy-start.20 = (bf16[8,2,32,2048]{3,2,1,0:T(8,128)(2,1)S(1)}, bf16[8,2,32,2048]{3,2,1,0:T(8,128)(2,1)}, u32[]{:S(2)}) copy-start(bf16[8,2,32,2048]{3,2,1,0:T(8,128)(2,1)} %copy-done.19) | copy-start | bytes 6291460
  683.9 90.2 %copy-start.24 = (bf16[8,2,32,2048]{3,2,1,0:T(8,128)(2,1)S(1)}, bf16[8,2,32,2048]{3,2,1,0:T(8,128)(2,1)}, u32[]{:S(2)}) copy-start(bf16[8,2,32,2048]{3,2,1,0:T(8,128)(2,1)} %copy-done.23) | copy-start | bytes 6291460
  780.0 91.8 %copy-start.26 = (bf16[8,2,32,2048]{3,2,1,0:T(8,128)(2,1)S(1)}, bf16[8,2,32,2048]{3,2,1,0:T(8,128)(2,1)}, u32[]{:S(2)}) copy-start(bf16[8,2,32,2048]{3,2,1,0:T(8,128)(2,1)} %copy-done.25) | copy-start | bytes 6291460
  877.7 90.2 %copy-start.28 = (bf16[8,2,32,2048]{3,2,1,0:T(8,128)(2,1)S(1)}, bf16[8,2,32,2048]{3,2,1,0:T(8,128)(2,1)}, u32[]{:S(2)}) copy-start(bf16[8,2,32,2048]{3,2,1,0:T(8,128)(2,1)} %copy-done.27) | copy-start | bytes 6291460
  973.8 91.8 %copy-start.30 = (bf16[8,2,32,2048]{3,2,1,0:T(8,128)(2,1)S(1)}, bf16[8,2,32,2048]{3,2,1,0:T(8,128)(2,1)}, u32[]{:S(2)}) copy-start(bf16[8,2,32,2048]{3,2,1,0:T(8,128)(2,1)} %copy-done.29) | copy-start | bytes 6291460
  1071.5 76.7 %copy-start.32 = (bf16[8,2,32,2048]{3,2,1,0:T(8,128)(2,1)S(1)}, bf16[8,2,32,2048]{3,2,1,0:T(8,128)(2,1)}, u32[]{:S(2)}) copy-start(bf16[8,2,32,2048]{3,2,1,0:T(8,128)(2,1)} %copy-done.31) | copy-start | bytes 6291460
  1154.1 78.6 %copy-start.34 = (bf16[8,2,32,2048]{3,2,1,0:T(8,128)(2,1)S(1)}, bf16[8,2,32,2048]{3,2,1,0:T(8,128)(2,1)}, u32[]{:S(2)}) copy-start(bf16[8,2,32,2048]{3,2,1,0:T(8,128)(2,1)} %copy-done.33) | copy-start | bytes 6291460
  1238.7 91.9 %copy-start.36 = (bf16[8,2,32,2048]{3,2,1,0:T(8,128)(2,1)S(1)}, bf16[8,2,32,2048]{3,2,1,0:T(8,128)(2,1)}, u32[]{:S(2)}) copy-start(bf16[8,2,32,2048]{3,2,1,0:T(8,128)(2,1)} %copy-done.35) | copy-start | bytes 6291460
  1336.4 91.8 %copy-start.38 = (bf16[8,2,32,2048]{3,2,1,0:T(8,128)(2,1)S(1)}, bf16[8,2,32,2048]{3,2,1,0:T(8,128)(2,1)}, u32[]{:S(2)}) copy-start(bf16[8,2,32,2048]{3,2,1,0:T(8,128)(2,1)} %copy-done.37) | copy-start | bytes 6291460
  (24 other events, 190.4 us)
Sparse Core Ops, SparseCore 0:
  2008.2 94.6 reduce-scatter.3
